TPU v7x, 32 devices: a whole 2x2x4 slice. The times are simulated.
32 devices in a mesh: dp: 32 (over z, y, x, core).
Axes of the slice: x: 2, y: 2, z: 4, core: 2. Of those that a mesh axis runs over, the one named last changes fastest.
Arguments:
- tokens: bfloat16 [192, 2, 197, 384], P('dp'), may hold values from -60 to 60
- counts: int32 [192], P('dp'), may hold values from 1 to 2, as said below
- cotangent: float32 [192, 2, 197, 384], P('dp'), may hold values from -6 to 6
- norm_gain: float32 [2, 2, 384], P(None, None, 'dp'), may hold values from 0.5 to 1.5
- bias_rows: float32 [2, 6, 384], P(None, None, 'dp'), may hold values from -1.8 to 1.8
- up_bias: float32 [2, 1536], P(None, 'dp'), may hold values from -1.8 to 1.8
- qkv_weight: float32 [2, 384, 1152], P(None, 'dp'), may hold values from -12 to 12
- out_weight: float32 [2, 384, 384], P(None, 'dp'), may hold values from -1.25 to 1.25
- up_weight: float32 [2, 384, 1536], P(None, 'dp'), may hold values from -0.3125 to 0.3125
- down_weight: float32 [2, 1536, 384], P(None, 'dp'), may hold values from -0.15625 to 0.15625
- first_norm_gain: float32 [2, 2, 384], P(None, None, 'dp'), may hold values from -0.06 to 0.06
- first_bias_rows: float32 [2, 6, 384], P(None, None, 'dp'), may hold values from -0.06 to 0.06
- first_up_bias: float32 [2, 1536], P(None, 'dp'), may hold values from -0.06 to 0.06
- first_qkv_weight: float32 [2, 384, 1152], P(None, 'dp'), may hold values from -0.06 to 0.06
- first_out_weight: float32 [2, 384, 384], P(None, 'dp'), may hold values from -0.06 to 0.06
- first_up_weight: float32 [2, 384, 1536], P(None, 'dp'), may hold values from -0.06 to 0.06
- first_down_weight: float32 [2, 1536, 384], P(None, 'dp'), may hold values from -0.06 to 0.06
- second_norm_gain: float32 [2, 2, 384], P(None, None, 'dp'), may hold values from 1e-05 to 0.001
- second_bias_rows: float32 [2, 6, 384], P(None, None, 'dp'), may hold values from 1e-05 to 0.001
- second_up_bias: float32 [2, 1536], P(None, 'dp'), may hold values from 1e-05 to 0.001
- second_qkv_weight: float32 [2, 384, 1152], P(None, 'dp'), may hold values from 1e-05 to 0.001
- second_out_weight: float32 [2, 384, 384], P(None, 'dp'), may hold values from 1e-05 to 0.001
- second_up_weight: float32 [2, 384, 1536], P(None, 'dp'), may hold values from 1e-05 to 0.001
- second_down_weight: float32 [2, 1536, 384], P(None, 'dp'), may hold values from 1e-05 to 0.001
Outputs:
- block_out: float32 [192, 2, 197, 384], P('dp')
- input_grad: float32 [192, 2, 197, 384], P('dp')
- grad_norm_gain: float32 [2, 2, 384], P(None, None, 'dp')
- grad_bias_rows: float32 [2, 6, 384], P(None, None, 'dp')
- grad_up_bias: float32 [2, 1536], P(None, 'dp')
- grad_qkv_weight: float32 [2, 384, 1152], P(None, 'dp')
- grad_out_weight: float32 [2, 384, 384], P(None, 'dp')
- grad_up_weight: float32 [2, 384, 1536], P(None, 'dp')
- grad_down_weight: float32 [2, 1536, 384], P(None, 'dp')
- new_norm_gain: float32 [2, 2, 384], P(None, None, 'dp')
- new_bias_rows: float32 [2, 6, 384], P(None, None, 'dp')
- new_up_bias: float32 [2, 1536], P(None, 'dp')
- new_qkv_weight: float32 [2, 384, 1152], P(None, 'dp')
- new_out_weight: float32 [2, 384, 384], P(None, 'dp')
- new_up_weight: float32 [2, 384, 1536], P(None, 'dp')
- new_down_weight: float32 [2, 1536, 384], P(None, 'dp')
- new_first_norm_gain: float32 [2, 2, 384], P(None, None, 'dp')
- new_first_bias_rows: float32 [2, 6, 384], P(None, None, 'dp')
- new_first_up_bias: float32 [2, 1536], P(None, 'dp')
- new_first_qkv_weight: float32 [2, 384, 1152], P(None, 'dp')
- new_first_out_weight: float32 [2, 384, 384], P(None, 'dp')
- new_first_up_weight: float32 [2, 384, 1536], P(None, 'dp')
- new_first_down_weight: float32 [2, 1536, 384], P(None, 'dp')
- new_second_norm_gain: float32 [2, 2, 384], P(None, None, 'dp')
- new_second_bias_rows: float32 [2, 6, 384], P(None, None, 'dp')
- new_second_up_bias: float32 [2, 1536], P(None, 'dp')
- new_second_qkv_weight: float32 [2, 384, 1152], P(None, 'dp')
- new_second_out_weight: float32 [2, 384, 384], P(None, 'dp')
- new_second_up_weight: float32 [2, 384, 1536], P(None, 'dp')
- new_second_down_weight: float32 [2, 1536, 384], P(None, 'dp')
Inputs may be any that keep to these rules, and one draw needn't show every extreme that they name: counts[g] images fill group g: slot 0 always, slot 1 only when counts[g] is 2; every draw has groups of both kinds.
All inputs are finite; a program needn't handle non-finite values.
Results may differ from a plain program's by a relative error of at most 0.02.
The roundings to bfloat16 on the way count: a program that leaves them out, or rounds other values in their place, can miss the bound.
Values may be sent and summed in bfloat16 or wider, within the bound.
No kernel may reach another device: no remote copies, remote signals or barrier semaphores. Data moves between devices by JAX's collectives and lax.ppermute only.
A program may use at most 320 MiB of HBM per device.

v0:
```python
import jax
import jax.numpy as jnp
from jax import lax
from jax.sharding import PartitionSpec as P

HD = 64
STEP = 3
BETA_ONE = 0.9
BETA_TWO = 0.95
LEARN_RATE = 0.02
DECAY = 0.05
ADAM_EPS = 1e-08
NORM_EPS = 1e-06


def mixed(form, left, right):
    return jnp.einsum(form, left, right, preferred_element_type=jnp.float32)


def cross_rows(left, right):
    return lax.dot_general(
        left, right, (((0,), (0,)), ((), ())), preferred_element_type=jnp.float32
    )


def back_dot(left, weight):
    return lax.dot_general(
        left, weight, (((1,), (1,)), ((), ())), preferred_element_type=jnp.float32
    )


def normalize(rows, gain, shift):
    center = rows - jnp.mean(rows, axis=-1, keepdims=True)
    rstd = lax.rsqrt(jnp.mean(center * center, axis=-1, keepdims=True) + NORM_EPS)
    normed = center * rstd
    return (normed * gain + shift, normed, rstd)


def norm_back(grad_in, gain, normed, rstd):
    scaled = grad_in * gain
    return rstd * (
        scaled
        - jnp.mean(scaled, axis=-1, keepdims=True)
        - normed * jnp.mean(scaled * normed, axis=-1, keepdims=True)
    )


def gelu_value(pre_act):
    return 0.5 * pre_act * (1.0 + lax.erf(pre_act * 0.7071067811865476))


def gelu_slope(pre_act):
    return (
        0.5 * (1.0 + lax.erf(pre_act * 0.7071067811865476))
        + pre_act * jnp.exp(-0.5 * pre_act * pre_act) * 0.3989422804014327
    )


def forward_layer(resid, weights, images, seq_len, head_size):
    gain_rows, shift_rows, up_shift, qkv_w, out_w, up_w, down_w = weights
    width = resid.shape[1]
    heads = width // head_size
    scale = head_size ** (-0.5)
    gains = gain_rows.astype(jnp.float32)
    shifts = shift_rows.astype(jnp.float32)
    first_f, normed_one, rstd_one = normalize(resid, gains[0], shifts[0])
    first_in = first_f.astype(jnp.bfloat16)
    proj = jnp.dot(first_in, qkv_w, preferred_element_type=jnp.float32)
    query = (
        ((proj[:, :width] + shifts[1]) * scale)
        .astype(jnp.bfloat16)
        .reshape(images, seq_len, heads, head_size)
    )
    keys = (
        proj[:, width : 2 * width].astype(jnp.bfloat16).reshape(images, seq_len, heads, head_size)
    )
    values = (
        (proj[:, 2 * width :] + shifts[2])
        .astype(jnp.bfloat16)
        .reshape(images, seq_len, heads, head_size)
    )
    scores = mixed("nqhd,nkhd->nhqk", query, keys)
    top = jnp.max(scores, axis=-1, keepdims=True)
    expo = jnp.exp(scores - top)
    total = jnp.sum(expo, axis=-1, keepdims=True)
    logsum = top + jnp.log(total)
    probs = (expo / total).astype(jnp.bfloat16)
    context = mixed("nhqk,nkhd->nqhd", probs, values).reshape(-1, width).astype(jnp.bfloat16)
    hidden_res = resid + jnp.dot(context, out_w, preferred_element_type=jnp.float32) + shifts[3]
    second_f, normed_two, rstd_two = normalize(hidden_res, gains[1], shifts[4])
    second_in = second_f.astype(jnp.bfloat16)
    pre_act = jnp.dot(second_in, up_w, preferred_element_type=jnp.float32) + up_shift.astype(
        jnp.float32
    )
    activ = gelu_value(pre_act).astype(jnp.bfloat16)
    result = hidden_res + jnp.dot(activ, down_w, preferred_element_type=jnp.float32) + shifts[5]
    saved = (
        first_in,
        normed_one,
        rstd_one,
        query,
        keys,
        values,
        logsum,
        context,
        normed_two,
        rstd_two,
        second_in,
        pre_act,
        activ,
    )
    return (result, saved)


def backward_layer(grad_out, weights, saved, head_size):
    gain_rows, shift_rows, up_shift, qkv_w, out_w, up_w, down_w = weights
    (
        first_in,
        normed_one,
        rstd_one,
        query,
        keys,
        values,
        logsum,
        context,
        normed_two,
        rstd_two,
        second_in,
        pre_act,
        activ,
    ) = saved
    width = grad_out.shape[1]
    scale = head_size ** (-0.5)
    gains = gain_rows.astype(jnp.float32)
    grad_low = grad_out.astype(jnp.bfloat16)
    grad_down = cross_rows(activ, grad_low)
    shift_five = jnp.sum(grad_out, axis=0)
    dpre = back_dot(grad_low, down_w) * gelu_slope(pre_act)
    dpre_low = dpre.astype(jnp.bfloat16)
    grad_up = cross_rows(second_in, dpre_low)
    grad_upshift = jnp.sum(dpre, axis=0)
    dsecond = back_dot(dpre_low, up_w)
    gain_two = jnp.sum(dsecond * normed_two, axis=0)
    shift_four = jnp.sum(dsecond, axis=0)
    dres = grad_out + norm_back(dsecond, gains[1], normed_two, rstd_two)
    dres_low = dres.astype(jnp.bfloat16)
    grad_outw = cross_rows(context, dres_low)
    shift_three = jnp.sum(dres, axis=0)
    dctx = back_dot(dres_low, out_w).astype(jnp.bfloat16).reshape(query.shape)
    scores = mixed("nqhd,nkhd->nhqk", query, keys)
    probs = jnp.exp(scores - logsum)
    probs_low = probs.astype(jnp.bfloat16)
    dvals = mixed("nhqk,nqhd->nkhd", probs_low, dctx).reshape(-1, width)
    dprobs = mixed("nqhd,nkhd->nhqk", dctx, values)
    inner = jnp.sum(probs * dprobs, axis=-1, keepdims=True)
    dscore = (probs * (dprobs - inner)).astype(jnp.bfloat16)
    dquery = (mixed("nhqk,nkhd->nqhd", dscore, keys) * scale).reshape(-1, width)
    dkeys = mixed("nhqk,nqhd->nkhd", dscore, query).reshape(-1, width)
    shift_one = jnp.sum(dquery, axis=0)
    shift_two = jnp.sum(dvals, axis=0)
    dproj = jnp.concatenate([dquery, dkeys, dvals], axis=1).astype(jnp.bfloat16)
    grad_qkv = cross_rows(first_in, dproj)
    dfirst = back_dot(dproj, qkv_w)
    gain_one = jnp.sum(dfirst * normed_one, axis=0)
    shift_zero = jnp.sum(dfirst, axis=0)
    dinput = dres + norm_back(dfirst, gains[0], normed_one, rstd_one)
    grads = (
        jnp.stack([gain_one, gain_two]),
        jnp.stack([shift_zero, shift_one, shift_two, shift_three, shift_four, shift_five]),
        grad_upshift,
        grad_qkv,
        grad_outw,
        grad_up,
        grad_down,
    )
    return (dinput, grads)


def adam_update(grad_sum, weight, first, second, count_rows, decay_on):
    grad = grad_sum / count_rows
    first_new = BETA_ONE * first + (1.0 - BETA_ONE) * grad
    second_new = BETA_TWO * second + (1.0 - BETA_TWO) * grad * grad
    fix_one = 1.0 - BETA_ONE**STEP
    fix_two = 1.0 - BETA_TWO**STEP
    direction = first_new / fix_one / (jnp.sqrt(second_new / fix_two) + ADAM_EPS)
    if decay_on:
        direction = direction + DECAY * weight
    return (grad, weight - LEARN_RATE * direction, first_new, second_new)


def layer_slice(params, layer):
    return tuple((p[layer].astype(jnp.bfloat16) for p in params))


def fetch_layer(params, layer):
    gain_part, shift_part, upshift_part, qkv_part, outw_part, up_part, down_part = layer_slice(
        params, layer
    )
    return (
        lax.all_gather(gain_part, "dp", axis=1, tiled=True),
        lax.all_gather(shift_part, "dp", axis=1, tiled=True),
        lax.all_gather(upshift_part, "dp", axis=0, tiled=True),
        lax.all_gather(qkv_part, "dp", axis=0, tiled=True),
        lax.all_gather(outw_part, "dp", axis=0, tiled=True),
        lax.all_gather(up_part, "dp", axis=0, tiled=True),
        lax.all_gather(down_part, "dp", axis=0, tiled=True),
    )


def fetch_again(params, layer):
    gain_part, shift_part, upshift_part, qkv_part, outw_part, up_part, down_part = layer_slice(
        params, layer
    )
    return (
        lax.all_gather(gain_part, "dp", axis=1, tiled=True),
        lax.all_gather(shift_part, "dp", axis=1, tiled=True),
        lax.all_gather(upshift_part, "dp", axis=0, tiled=True),
        lax.all_gather(qkv_part, "dp", axis=0, tiled=True),
        lax.all_gather(outw_part, "dp", axis=0, tiled=True),
        lax.all_gather(up_part, "dp", axis=0, tiled=True),
        lax.all_gather(down_part, "dp", axis=0, tiled=True),
    )


def reduce_layer(grads):
    gain_term, shift_term, upshift_term, qkv_term, outw_term, up_term, down_term = grads
    return (
        lax.psum_scatter(gain_term, "dp", scatter_dimension=1, tiled=True),
        lax.psum_scatter(shift_term, "dp", scatter_dimension=1, tiled=True),
        lax.psum_scatter(upshift_term, "dp", scatter_dimension=0, tiled=True),
        lax.psum_scatter(qkv_term, "dp", scatter_dimension=0, tiled=True),
        lax.psum_scatter(outw_term, "dp", scatter_dimension=0, tiled=True),
        lax.psum_scatter(up_term, "dp", scatter_dimension=0, tiled=True),
        lax.psum_scatter(down_term, "dp", scatter_dimension=0, tiled=True),
    )


def body(
    tokens,
    counts,
    cotangent,
    norm_gain,
    bias_rows,
    up_bias,
    qkv_weight,
    out_weight,
    up_weight,
    down_weight,
    first_norm_gain,
    first_bias_rows,
    first_up_bias,
    first_qkv_weight,
    first_out_weight,
    first_up_weight,
    first_down_weight,
    second_norm_gain,
    second_bias_rows,
    second_up_bias,
    second_qkv_weight,
    second_out_weight,
    second_up_weight,
    second_down_weight,
):
    params = (norm_gain, bias_rows, up_bias, qkv_weight, out_weight, up_weight, down_weight)
    firsts = (
        first_norm_gain,
        first_bias_rows,
        first_up_bias,
        first_qkv_weight,
        first_out_weight,
        first_up_weight,
        first_down_weight,
    )
    seconds = (
        second_norm_gain,
        second_bias_rows,
        second_up_bias,
        second_qkv_weight,
        second_out_weight,
        second_up_weight,
        second_down_weight,
    )
    groups = tokens.shape[0]
    seq_len = tokens.shape[2]
    width = tokens.shape[3]
    images = 2 * groups
    layers = qkv_weight.shape[0]
    live = jnp.stack([jnp.ones_like(counts), (counts == 2).astype(jnp.int32)], axis=1).astype(
        jnp.float32
    )
    live_rows = jnp.broadcast_to(live[:, :, None], (groups, 2, seq_len)).reshape(-1, 1)
    resid = tokens.astype(jnp.float32).reshape(-1, width)
    kept = []
    saved_all = []
    for layer in range(layers):
        gathered = fetch_layer(params, layer)
        kept.append(gathered)
        resid, saved = forward_layer(resid, gathered, images, seq_len, HD)
        saved_all.append(saved)
    block_out = (resid * live_rows).reshape(tokens.shape)
    grad = cotangent.reshape(-1, width) * live_rows
    reduced = [None] * layers
    for layer in reversed(range(layers)):
        weights = fetch_again(params, layer)
        grad, local = backward_layer(grad, weights, saved_all[layer], HD)
        reduced[layer] = reduce_layer(local)
    sums = tuple((jnp.stack([reduced[layer][i] for layer in range(layers)]) for i in range(7)))
    input_grad = (grad * live_rows).reshape(tokens.shape)
    count_rows = float(lax.axis_size("dp") * groups * 2 * seq_len)
    results = [
        adam_update(sums[i], params[i], firsts[i], seconds[i], count_rows, i >= 3) for i in range(7)
    ]
    return (
        block_out,
        input_grad,
        results[0][0],
        results[1][0],
        results[2][0],
        results[3][0],
        results[4][0],
        results[5][0],
        results[6][0],
        results[0][1],
        results[1][1],
        results[2][1],
        results[3][1],
        results[4][1],
        results[5][1],
        results[6][1],
        results[0][2],
        results[1][2],
        results[2][2],
        results[3][2],
        results[4][2],
        results[5][2],
        results[6][2],
        results[0][3],
        results[1][3],
        results[2][3],
        results[3][3],
        results[4][3],
        results[5][3],
        results[6][3],
    )


def solution(mesh):
    return jax.shard_map(
        body,
        mesh=mesh,
        in_specs=(
            P("dp", None, None, None),
            P("dp"),
            P("dp", None, None, None),
            P(None, None, "dp"),
            P(None, None, "dp"),
            P(None, "dp"),
            P(None, "dp", None),
            P(None, "dp", None),
            P(None, "dp", None),
            P(None, "dp", None),
            P(None, None, "dp"),
            P(None, None, "dp"),
            P(None, "dp"),
            P(None, "dp", None),
            P(None, "dp", None),
            P(None, "dp", None),
            P(None, "dp", None),
            P(None, None, "dp"),
            P(None, None, "dp"),
            P(None, "dp"),
            P(None, "dp", None),
            P(None, "dp", None),
            P(None, "dp", None),
            P(None, "dp", None),
        ),
        out_specs=(
            P("dp", None, None, None),
            P("dp", None, None, None),
            P(None, None, "dp"),
            P(None, None, "dp"),
            P(None, "dp"),
            P(None, "dp", None),
            P(None, "dp", None),
            P(None, "dp", None),
            P(None, "dp", None),
            P(None, None, "dp"),
            P(None, None, "dp"),
            P(None, "dp"),
            P(None, "dp", None),
            P(None, "dp", None),
            P(None, "dp", None),
            P(None, "dp", None),
            P(None, None, "dp"),
            P(None, None, "dp"),
            P(None, "dp"),
            P(None, "dp", None),
            P(None, "dp", None),
            P(None, "dp", None),
            P(None, "dp", None),
            P(None, None, "dp"),
            P(None, None, "dp"),
            P(None, "dp"),
            P(None, "dp", None),
            P(None, "dp", None),
            P(None, "dp", None),
            P(None, "dp", None),
        ),
        check_vma=False,
    )
```

profile of v0, /device:TPU:0, one launch (start us, length us, event | category | flops | bytes accessed | tf_op | source)
XLA Modules:
  0.0 1307.4 jit_solution(14078467237861299334)
XLA Ops:
  15.5 16.8 %multiply_reduce_fusion.14 = f32[6,2,197]{1,2,0:T(8,128)S(1)} fusion(f32[6,2,197]{1,2,0:T(8,128)S(1)} %broadcast_multiply_fusion, bf16[6,2,197,384]{3,1,2,0:T(2,128)(2,1)S(1)} %copy-done.20), kind=kLoop, calls=%fused_computation.98 | loop fusion | flops 3628740 | bytes 1834464 | tf_op jit(solution)/shard_map/reduce_sum | solution.py:34
  42.4 42.7 %all-reduce.22 = (bf16[1536]{0:T(1024)(128)(2,1)S(1)}, bf16[1536]{0:T(1024)(128)(2,1)S(1)}) all-reduce(bf16[1536]{0:T(1024)(128)(2,1)S(1)} %dynamic-update-slice, bf16[1536]{0:T(1024)(128)(2,1)S(1)} %dynamic-update-slice.1), channel_id=7, replica_groups=mesh['dp'=32] {'dp'}, use_global_device_ids=true, to_apply=%add.1 | all-reduce | flops 3072 | bytes 12288
  86.4 40.9 %all-gather.7 = bf16[1,2,384]{1,0,2:T(2,128)(2,1)S(1)} all-gather(bf16[1,2,12]{1,0,2:T(2,128)(2,1)S(1)} %get-tuple-element.278), channel_id=9, replica_groups=mesh['dp'=32] {'dp'}, dimensions={2}, use_global_device_ids=true | all-gather | bytes 1584 | tf_op jit(solution)/shard_map/all_gather | solution.py:200
  129.2 37.4 %all-gather.8 = bf16[1,6,384]{1,0,2:T(2,128)(2,1)S(1)} all-gather(bf16[1,6,12]{1,0,2:T(2,128)(2,1)S(1)} %get-tuple-element.280), channel_id=10, replica_groups=mesh['dp'=32] {'dp'}, dimensions={2}, use_global_device_ids=true | all-gather | bytes 4752 | tf_op jit(solution)/shard_map/all_gather | solution.py:201
  166.7 8.8 slice_reduce_fusion
  175.5 38.6 %all-gather = bf16[1,2,384]{1,0,2:T(2,128)(2,1)S(1)} all-gather(bf16[1,2,12]{1,0,2:T(2,128)(2,1)S(1)} %get-tuple-element.279), channel_id=2, replica_groups=mesh['dp'=32] {'dp'}, dimensions={2}, use_global_device_ids=true | all-gather | bytes 1584 | tf_op jit(solution)/shard_map/all_gather | solution.py:200
  216.1 37.6 %all-gather.1 = bf16[1,6,384]{1,0,2:T(2,128)(2,1)S(1)} all-gather(bf16[1,6,12]{1,0,2:T(2,128)(2,1)S(1)} %get-tuple-element.281), channel_id=3, replica_groups=mesh['dp'=32] {'dp'}, dimensions={2}, use_global_device_ids=true | all-gather | bytes 4752 | tf_op jit(solution)/shard_map/all_gather | solution.py:201
  253.9 8.3 slice_reduce_fusion.8
  262.3 42.3 %all-gather.10 = bf16[1,384,384]{2,0,1:T(2,128)(2,1)} all-gather(bf16[1,12,384]{2,0,1:T(2,128)(2,1)S(1)} %get-tuple-element.275), channel_id=12, replica_groups=mesh['dp'=32] {'dp'}, dimensions={1}, use_global_device_ids=true | all-gather | bytes 304128 | tf_op jit(solution)/shard_map/all_gather | solution.py:204
  304.6 40.9 %all-gather.3 = bf16[1,384,384]{2,0,1:T(2,128)(2,1)} all-gather(bf16[1,12,384]{2,0,1:T(2,128)(2,1)S(1)} %get-tuple-element.276), channel_id=5, replica_groups=mesh['dp'=32] {'dp'}, dimensions={1}, use_global_device_ids=true | all-gather | bytes 304128 | tf_op jit(solution)/shard_map/all_gather | solution.py:204
  346.0 45.5 %all-gather.9 = bf16[1,384,1152]{2,0,1:T(2,128)(2,1)} all-gather(bf16[1,12,1152]{2,0,1:T(2,128)(2,1)S(1)} %get-tuple-element.272), channel_id=11, replica_groups=mesh['dp'=32] {'dp'}, dimensions={1}, use_global_device_ids=true | all-gather | bytes 912384 | tf_op jit(solution)/shard_map/all_gather | solution.py:203
  391.6 42.6 %all-gather.2 = bf16[1,384,1152]{2,0,1:T(2,128)(2,1)S(1)} all-gather(bf16[1,12,1152]{2,0,1:T(2,128)(2,1)S(1)} %get-tuple-element.273), channel_id=4, replica_groups=mesh['dp'=32] {'dp'}, dimensions={1}, use_global_device_ids=true | all-gather | bytes 912384 | tf_op jit(solution)/shard_map/all_gather | solution.py:203
  442.6 5.7 fusion.70
  456.4 6.4 copy.367
  467.5 5.0 copy.368
  472.6 6.8 reshape.364
  479.4 6.4 copy.369
  485.8 9.0 fusion.132
  494.9 8.7 fusion.16
  504.2 8.2 convert_bitcast_fusion.3
  515.6 5.2 convert_element_type.199
  527.9 12.0 multiply_convert_fusion.3
  539.9 8.6 fusion.134
  562.9 6.6 copy.375
  574.2 5.0 copy.376
  579.2 6.6 reshape.367
  585.8 6.3 copy.377
  592.1 9.0 fusion.135
  601.2 8.6 fusion.17
  609.8 8.1 convert_bitcast_fusion.2
  621.2 6.5 convert_element_type.218
  634.7 11.7 multiply_convert_fusion.2
  646.5 12.4 fusion.137
  663.8 5.2 multiply_reduce_fusion.2
  676.4 6.6 reshape.370
  682.9 6.4 copy.383
  689.4 11.3 bitcast_convert_fusion.2
  700.7 10.0 multiply_reduce_fusion.1
  710.7 10.7 multiply_convert_fusion.1
  732.9 6.2 reshape.290
  742.4 6.3 reshape.288
  765.7 6.4 multiply_reduce_fusion.3
  774.7 14.5 %fusion.138 = (f32[1536]{0:T(1024)}, bf16[2364,1536]{1,0:T(8,128)(2,1)S(1)}) fusion(f32[2364,1536]{1,0:T(8,128)} %get-tuple-element.289, bf16[1,1536,384]{2,1,0:T(8,128)(2,1)S(1)} %copy-done.128, f32[2364,384]{1,0:T(8,128)S(1)} %get-tuple-element.257), kind=kOutput, calls=%fused_computation.286 | convolution fusion | flops 2829536256 | bytes 26603520 | tf_op jit(solution)/shard_map/dot_general | solution.py:27
  794.2 5.2 multiply_reduce_fusion.4
  809.9 5.1 copy.395
  815.0 10.8 bitcast_convert_fusion
  825.8 10.0 multiply_reduce_fusion
  835.8 10.9 multiply_convert_fusion
  857.5 6.1 reshape.294
  866.7 6.1 reshape.292
  876.0 5.0 reshape.293
  891.4 135.7 %fusion.113 = (f32[16,1152]{1,0:T(8,128)}, f32[16,1152]{1,0:T(8,128)}, f32[16,384]{1,0:T(8,128)}, f32[16,384]{1,0:T(8,128)}, f32[16,1536]{1,0:T(8,128)}, /*index=5*/f32[16,1536]{1,0:T(8,128)}) fusion(f32[384,1152]{1,0:T(8,128)} %fusion.112, f32[384,1152]{1,0:T(8,128)} %fusion.111, f32[384,384]{1,0:T(8,128)S(1)} %copy-done.40, ...), kind=kCustom, calls=%all-reduce-scatter.6 | all-reduce-scatter fusion | flops 3145729 | bytes 9830400
  1033.4 9.9 fusion.110
  1053.1 10.5 multiply_reduce_fusion.5
  1063.6 6.4 collective-permute-start.23
  1073.6 39.6 %all-reduce.21 = (f32[2,384]{1,0:T(2,128)S(1)}, f32[2,384]{1,0:T(2,128)S(1)}, f32[6,384]{1,0:T(8,128)S(1)}, f32[6,384]{1,0:T(8,128)S(1)}, f32[1536]{0:T(1024)S(1)}, /*index=5*/f32[1536]{0:T(1024)S(1)}) all-reduce(f32[2,384]{1,0:T(2,128)S(1)} %pad_maximum_fusion.6, ...), channel_id=17, replica_groups=mesh['dp'=32] {'dp'}, use_global_device_ids=true, to_apply=%region_27.0.clone | all-reduce | flops 9216 | bytes 73728
  1113.4 9.9 fusion.58
  1123.4 8.4 add_multiply_fusion
  1131.9 9.1 fusion.32
  1182.7 5.8 copy.422
  1194.7 5.8 copy.423
  1254.3 5.4 collective-permute-start.41
  1261.1 7.0 collective-permute-start.38
  1288.6 6.3 concatenate.14
  (551 shorter events, 322.4 us)
Async XLA Ops:
  7.2 520.6 %all-gather.19.cloned.1.call-start = ((), (), s32[]{:S(2)}) async-start(), calls=%async_computation.4 | async-start | bytes 2433024 | tf_op jit(solution)/shard_map/all_gather | solution.py:205
  9.1 530.8 %all-gather.21.cloned.1.call-start = ((), (), s32[]{:S(2)}) async-start(), calls=%async_computation.5 | async-start | bytes 1216512 | tf_op jit(solution)/shard_map/all_gather | solution.py:206
  10.8 623.9 %all-gather.23.cloned.1.call-start = ((), (), s32[]{:S(2)}) async-start(), calls=%async_computation.6 | async-start | bytes 2433024 | tf_op jit(solution)/shard_map/all_gather | solution.py:205
  11.5 634.9 %all-gather.25.cloned.1.call-start = ((), (), s32[]{:S(2)}) async-start(), calls=%async_computation.7 | async-start | bytes 1216512 | tf_op jit(solution)/shard_map/all_gather | solution.py:206
  12.1 1286.2 %reduce-scatter.21.cloned.1.call-start = ((), (), s32[]{:S(2)}) async-start(), calls=%async_computation.3 | async-start | bytes 2433024 | tf_op jit(solution)/shard_map/reduce_scatter | solution.py:234
  129.2 420.3 %copy-start.90 = (f32[384]{0:T(512)}, f32[384]{0:T(512)S(1)}, u32[]{:S(2)}) copy-start(f32[384]{0:T(512)S(1)} %get-tuple-element.203) | copy-start | bytes 4612
  175.5 373.9 %copy-start.96 = (f32[384]{0:T(512)}, f32[384]{0:T(512)S(1)}, u32[]{:S(2)}) copy-start(f32[384]{0:T(512)S(1)} %get-tuple-element.201) | copy-start | bytes 4612
  216.1 226.5 %copy-start.88 = (f32[384]{0:T(512)}, f32[384]{0:T(512)S(1)}, u32[]{:S(2)}) copy-start(f32[384]{0:T(512)S(1)} %get-tuple-element.211) | copy-start | bytes 4612
  216.1 311.7 %copy-start.98 = (f32[384]{0:T(512)}, f32[384]{0:T(512)S(1)}, u32[]{:S(2)}) copy-start(f32[384]{0:T(512)S(1)} %get-tuple-element.210) | copy-start | bytes 4612
  262.3 180.3 %copy-start.94 = (f32[384]{0:T(512)}, f32[384]{0:T(512)S(1)}, u32[]{:S(2)}) copy-start(f32[384]{0:T(512)S(1)} %get-tuple-element.209) | copy-start | bytes 4612
  262.3 265.6 %copy-start.111 = (f32[384]{0:T(512)}, f32[384]{0:T(512)S(1)}, u32[]{:S(2)}) copy-start(f32[384]{0:T(512)S(1)} %get-tuple-element.205) | copy-start | bytes 4612
  345.5 97.1 %copy-start.60 = (f32[2364]{0:T(1024)}, f32[2364]{0:T(1024)S(1)}, u32[]{:S(2)}) copy-start(f32[2364]{0:T(1024)S(1)} %div.214) | copy-start | bytes 28372
  346.0 96.6 %copy-start.62 = (f32[2364]{0:T(1024)}, f32[2364]{0:T(1024)S(1)}, u32[]{:S(2)}) copy-start(f32[2364]{0:T(1024)S(1)} %rsqrt.36) | copy-start | bytes 28372
  1027.9 119.2 %collective-permute-start.30 = (f32[16,384]{1,0:T(8,128)}, f32[16,384]{1,0:T(8,128)S(1)}, u32[]{:S(2)}, u32[]{:S(2)}) collective-permute-start(f32[16,384]{1,0:T(8,128)} %get-tuple-element.228), channel_id=1, source_target_pairs={{0,7},{1,8},{2,9},{3,10},{4,11},{5,12},{6,13},{7,14},{8,15},{9,16}... | collective-permute-start | bytes 73736
  1029.2 121.5 %collective-permute-start.29 = (f32[16,384]{1,0:T(8,128)}, f32[16,384]{1,0:T(8,128)S(1)}, u32[]{:S(2)}, u32[]{:S(2)}) collective-permute-start(f32[16,384]{1,0:T(8,128)} %get-tuple-element.228), channel_id=1, source_target_pairs={{0,6},{1,7},{2,8},{3,9},{4,10},{5,11},{6,12},{7,13},{8,14},{9,15},... | collective-permute-start | bytes 73736
  1031.8 122.8 %collective-permute-start.28 = (f32[16,384]{1,0:T(8,128)}, f32[16,384]{1,0:T(8,128)S(1)}, u32[]{:S(2)}, u32[]{:S(2)}) collective-permute-start(f32[16,384]{1,0:T(8,128)} %get-tuple-element.228), channel_id=1, source_target_pairs={{0,5},{1,6},{2,7},{3,8},{4,9},{5,10},{6,11},{7,12},{8,13},{9,14},{... | collective-permute-start | bytes 73736
  1043.4 254.9 %reduce-scatter.19.cloned.1.call-start = ((), (), s32[]{:S(2)}) async-start(), calls=%async_computation.2 | async-start | bytes 2433024 | tf_op jit(solution)/shard_map/reduce_scatter | solution.py:234
  1063.6 78.1 %collective-permute-start.23 = (f32[12,384]{1,0:T(8,128)S(1)}, f32[12,384]{1,0:T(8,128)S(1)}, u32[]{:S(2)}, u32[]{:S(2)}) collective-permute-start(f32[12,384]{1,0:T(8,128)S(1)} %slice.226), channel_id=1, source_target_pairs={{0,8},{1,9},{2,10},{3,11},{4,12},{5,13},{6,14},{7,15},{8,16},{9,17... | collective-permute-start | bytes 55304
  1070.0 75.8 %collective-permute-start.31 = (f32[12,384]{1,0:T(8,128)S(1)}, f32[12,384]{1,0:T(8,128)S(1)}, u32[]{:S(2)}, u32[]{:S(2)}) collective-permute-start(f32[12,384]{1,0:T(8,128)S(1)} %slice.227), channel_id=1, source_target_pairs={{0,8},{1,9},{2,10},{3,11},{4,12},{5,13},{6,14},{7,15},{8,16},{9,17... | collective-permute-start | bytes 55304
  1141.7 17.4 %collective-permute-start.27 = (f32[16,384]{1,0:T(8,128)S(1)}, f32[16,384]{1,0:T(8,128)S(1)}, u32[]{:S(2)}, u32[]{:S(2)}) collective-permute-start(f32[16,384]{1,0:T(8,128)S(1)} %copy-done.59), channel_id=1, source_target_pairs={{0,4},{1,5},{2,6},{3,7},{4,8},{5,9},{6,10},{7,11},{8,12},{9,13},{1... | collective-permute-start | bytes 73736
  1145.8 15.6 %collective-permute-start.26 = (f32[16,384]{1,0:T(8,128)S(1)}, f32[16,384]{1,0:T(8,128)S(1)}, u32[]{:S(2)}, u32[]{:S(2)}) collective-permute-start(f32[16,384]{1,0:T(8,128)S(1)} %copy-done.59), channel_id=1, source_target_pairs={{0,3},{1,4},{2,5},{3,6},{4,7},{5,8},{6,9},{7,10},{8,11},{9,12},{10... | collective-permute-start | bytes 73736
  1147.1 16.2 %collective-permute-start.25 = (f32[16,384]{1,0:T(8,128)S(1)}, f32[16,384]{1,0:T(8,128)S(1)}, u32[]{:S(2)}, u32[]{:S(2)}) collective-permute-start(f32[16,384]{1,0:T(8,128)S(1)} %copy-done.59), channel_id=1, source_target_pairs={{0,2},{1,3},{2,4},{3,5},{4,6},{5,7},{6,8},{7,9},{8,10},{9,11},{10,... | collective-permute-start | bytes 73736
  1150.6 16.3 %collective-permute-start.24 = (f32[16,384]{1,0:T(8,128)S(1)}, f32[16,384]{1,0:T(8,128)S(1)}, u32[]{:S(2)}, u32[]{:S(2)}) collective-permute-start(f32[16,384]{1,0:T(8,128)S(1)} %copy-done.59), channel_id=1, source_target_pairs={{0,1},{1,2},{2,3},{3,4},{4,5},{5,6},{6,7},{7,8},{8,9},{9,10},{10,1... | collective-permute-start | bytes 73736
  1154.6 14.3 %collective-permute-start.22 = (f32[16,384]{1,0:T(8,128)S(1)}, f32[16,384]{1,0:T(8,128)S(1)}, u32[]{:S(2)}, u32[]{:S(2)}) collective-permute-start(f32[16,384]{1,0:T(8,128)S(1)} %copy-done.58), channel_id=1, source_target_pairs={{0,7},{1,8},{2,9},{3,10},{4,11},{5,12},{6,13},{7,14},{8,15},{9,16}... | collective-permute-start | bytes 73736
  1159.1 14.2 %collective-permute-start.21 = (f32[16,384]{1,0:T(8,128)S(1)}, f32[16,384]{1,0:T(8,128)S(1)}, u32[]{:S(2)}, u32[]{:S(2)}) collective-permute-start(f32[16,384]{1,0:T(8,128)S(1)} %copy-done.58), channel_id=1, source_target_pairs={{0,6},{1,7},{2,8},{3,9},{4,10},{5,11},{6,12},{7,13},{8,14},{9,15},... | collective-permute-start | bytes 73736
  1161.5 13.1 %collective-permute-start.20 = (f32[16,384]{1,0:T(8,128)S(1)}, f32[16,384]{1,0:T(8,128)S(1)}, u32[]{:S(2)}, u32[]{:S(2)}) collective-permute-start(f32[16,384]{1,0:T(8,128)S(1)} %copy-done.58), channel_id=1, source_target_pairs={{0,5},{1,6},{2,7},{3,8},{4,9},{5,10},{6,11},{7,12},{8,13},{9,14},{... | collective-permute-start | bytes 73736
  1163.4 12.6 collective-permute-start.19
  1166.9 34.5 %collective-permute-start.18 = (f32[16,384]{1,0:T(8,128)S(1)}, f32[16,384]{1,0:T(8,128)S(1)}, u32[]{:S(2)}, u32[]{:S(2)}) collective-permute-start(f32[16,384]{1,0:T(8,128)S(1)} %copy-done.58), channel_id=1, source_target_pairs={{0,3},{1,4},{2,5},{3,6},{4,7},{5,8},{6,9},{7,10},{8,11},{9,12},{10... | collective-permute-start | bytes 73736
  1168.8 35.4 %collective-permute-start.17 = (f32[16,384]{1,0:T(8,128)S(1)}, f32[16,384]{1,0:T(8,128)S(1)}, u32[]{:S(2)}, u32[]{:S(2)}) collective-permute-start(f32[16,384]{1,0:T(8,128)S(1)} %copy-done.58), channel_id=1, source_target_pairs={{0,2},{1,3},{2,4},{3,5},{4,6},{5,7},{6,8},{7,9},{8,10},{9,11},{10,... | collective-permute-start | bytes 73736
  1173.3 33.5 %collective-permute-start.16 = (f32[16,384]{1,0:T(8,128)S(1)}, f32[16,384]{1,0:T(8,128)S(1)}, u32[]{:S(2)}, u32[]{:S(2)}) collective-permute-start(f32[16,384]{1,0:T(8,128)S(1)} %copy-done.58), channel_id=1, source_target_pairs={{0,1},{1,2},{2,3},{3,4},{4,5},{5,6},{6,7},{7,8},{8,9},{9,10},{10,1... | collective-permute-start | bytes 73736
  1174.6 35.7 %collective-permute-start.7 = (f32[12,1152]{1,0:T(8,128)S(1)}, f32[12,1152]{1,0:T(8,128)S(1)}, u32[]{:S(2)}, u32[]{:S(2)}) collective-permute-start(f32[12,1152]{1,0:T(8,128)S(1)} %slice.224), channel_id=1, source_target_pairs={{0,8},{1,9},{2,10},{3,11},{4,12},{5,13},{6,14},{7,15},{8,16},{9,17... | collective-permute-start | bytes 165896
  1176.0 35.9 %collective-permute-start.15 = (f32[12,1152]{1,0:T(8,128)S(1)}, f32[12,1152]{1,0:T(8,128)S(1)}, u32[]{:S(2)}, u32[]{:S(2)}) collective-permute-start(f32[12,1152]{1,0:T(8,128)S(1)} %slice.225), channel_id=1, source_target_pairs={{0,8},{1,9},{2,10},{3,11},{4,12},{5,13},{6,14},{7,15},{8,16},{9,17... | collective-permute-start | bytes 165896
  1200.4 81.6 %copy-start.77 = (f32[2,12,1152]{2,0,1:T(2,128)S(1)}, f32[2,12,1152]{2,0,1:T(2,128)}, u32[]{:S(2)}) copy-start(f32[2,12,1152]{2,0,1:T(2,128)} %param.37) | copy-start | bytes 331780
  1200.4 81.6 %copy-start.78 = (f32[2,12,1152]{2,0,1:T(2,128)S(1)}, f32[2,12,1152]{2,0,1:T(2,128)}, u32[]{:S(2)}) copy-start(f32[2,12,1152]{2,0,1:T(2,128)} %param.44) | copy-start | bytes 331780
  1201.5 12.2 collective-permute-start.14
  1204.3 13.4 %collective-permute-start.13 = (f32[16,1152]{1,0:T(8,128)S(1)}, f32[16,1152]{1,0:T(8,128)S(1)}, u32[]{:S(2)}, u32[]{:S(2)}) collective-permute-start(f32[16,1152]{1,0:T(8,128)S(1)} %copy-done.50), channel_id=1, source_target_pairs={{0,6},{1,7},{2,8},{3,9},{4,10},{5,11},{6,12},{7,13},{8,14},{9,15},... | collective-permute-start | bytes 221192
  1206.8 12.1 collective-permute-start.12
  1210.4 11.7 collective-permute-start.11
  1212.0 11.5 collective-permute-start.10
  1213.7 12.3 collective-permute-start.9
  1217.7 9.7 collective-permute-start.8
  1219.0 11.2 collective-permute-start.6
  1222.1 11.2 collective-permute-start.5
  1223.4 11.2 collective-permute-start.4
  1226.0 13.7 %collective-permute-start.3 = (f32[16,1152]{1,0:T(8,128)S(1)}, f32[16,1152]{1,0:T(8,128)S(1)}, u32[]{:S(2)}, u32[]{:S(2)}) collective-permute-start(f32[16,1152]{1,0:T(8,128)S(1)} %copy-done.49), channel_id=1, source_target_pairs={{0,4},{1,5},{2,6},{3,7},{4,8},{5,9},{6,10},{7,11},{8,12},{9,13},{1... | collective-permute-start | bytes 221192
  1227.3 14.9 %collective-permute-start.2 = (f32[16,1152]{1,0:T(8,128)S(1)}, f32[16,1152]{1,0:T(8,128)S(1)}, u32[]{:S(2)}, u32[]{:S(2)}) collective-permute-start(f32[16,1152]{1,0:T(8,128)S(1)} %copy-done.49), channel_id=1, source_target_pairs={{0,3},{1,4},{2,5},{3,6},{4,7},{5,8},{6,9},{7,10},{8,11},{9,12},{10... | collective-permute-start | bytes 221192
  1230.2 13.7 %collective-permute-start.1 = (f32[16,1152]{1,0:T(8,128)S(1)}, f32[16,1152]{1,0:T(8,128)S(1)}, u32[]{:S(2)}, u32[]{:S(2)}) collective-permute-start(f32[16,1152]{1,0:T(8,128)S(1)} %copy-done.49), channel_id=1, source_target_pairs={{0,2},{1,3},{2,4},{3,5},{4,6},{5,7},{6,8},{7,9},{8,10},{9,11},{10,... | collective-permute-start | bytes 221192
  1233.3 12.2 collective-permute-start
  1234.6 13.5 %collective-permute-start.39 = (f32[12,1536]{1,0:T(8,128)S(1)}, f32[12,1536]{1,0:T(8,128)S(1)}, u32[]{:S(2)}, u32[]{:S(2)}) collective-permute-start(f32[12,1536]{1,0:T(8,128)S(1)} %slice.228), channel_id=1, source_target_pairs={{0,8},{1,9},{2,10},{3,11},{4,12},{5,13},{6,14},{7,15},{8,16},{9,17... | collective-permute-start | bytes 221192
  1239.7 14.6 %collective-permute-start.46 = (f32[16,1536]{1,0:T(8,128)S(1)}, f32[16,1536]{1,0:T(8,128)S(1)}, u32[]{:S(2)}, u32[]{:S(2)}) collective-permute-start(f32[16,1536]{1,0:T(8,128)S(1)} %copy-done.48), channel_id=1, source_target_pairs={{0,7},{1,8},{2,9},{3,10},{4,11},{5,12},{6,13},{7,14},{8,15},{9,16}... | collective-permute-start | bytes 294920
  1242.3 17.5 %collective-permute-start.45 = (f32[16,1536]{1,0:T(8,128)S(1)}, f32[16,1536]{1,0:T(8,128)S(1)}, u32[]{:S(2)}, u32[]{:S(2)}) collective-permute-start(f32[16,1536]{1,0:T(8,128)S(1)} %copy-done.48), channel_id=1, source_target_pairs={{0,6},{1,7},{2,8},{3,9},{4,10},{5,11},{6,12},{7,13},{8,14},{9,15},... | collective-permute-start | bytes 294920
  1243.8 17.2 %collective-permute-start.44 = (f32[16,1536]{1,0:T(8,128)S(1)}, f32[16,1536]{1,0:T(8,128)S(1)}, u32[]{:S(2)}, u32[]{:S(2)}) collective-permute-start(f32[16,1536]{1,0:T(8,128)S(1)} %copy-done.48), channel_id=1, source_target_pairs={{0,5},{1,6},{2,7},{3,8},{4,9},{5,10},{6,11},{7,12},{8,13},{9,14},{... | collective-permute-start | bytes 294920
  1245.5 22.6 %collective-permute-start.43 = (f32[16,1536]{1,0:T(8,128)S(1)}, f32[16,1536]{1,0:T(8,128)S(1)}, u32[]{:S(2)}, u32[]{:S(2)}) collective-permute-start(f32[16,1536]{1,0:T(8,128)S(1)} %copy-done.48), channel_id=1, source_target_pairs={{0,4},{1,5},{2,6},{3,7},{4,8},{5,9},{6,10},{7,11},{8,12},{9,13},{1... | collective-permute-start | bytes 294920
  1248.1 3.8 collective-permute-start.47
  1251.9 17.5 %collective-permute-start.42 = (f32[16,1536]{1,0:T(8,128)S(1)}, f32[16,1536]{1,0:T(8,128)S(1)}, u32[]{:S(2)}, u32[]{:S(2)}) collective-permute-start(f32[16,1536]{1,0:T(8,128)S(1)} %copy-done.48), channel_id=1, source_target_pairs={{0,3},{1,4},{2,5},{3,6},{4,7},{5,8},{6,9},{7,10},{8,11},{9,12},{10... | collective-permute-start | bytes 294920
  1254.3 17.0 %collective-permute-start.41 = (f32[16,1536]{1,0:T(8,128)S(1)}, f32[16,1536]{1,0:T(8,128)S(1)}, u32[]{:S(2)}, u32[]{:S(2)}) collective-permute-start(f32[16,1536]{1,0:T(8,128)S(1)} %copy-done.48), channel_id=1, source_target_pairs={{0,2},{1,3},{2,4},{3,5},{4,6},{5,7},{6,8},{7,9},{8,10},{9,11},{10,... | collective-permute-start | bytes 294920
  1259.7 14.1 %collective-permute-start.40 = (f32[16,1536]{1,0:T(8,128)S(1)}, f32[16,1536]{1,0:T(8,128)S(1)}, u32[]{:S(2)}, u32[]{:S(2)}) collective-permute-start(f32[16,1536]{1,0:T(8,128)S(1)} %copy-done.48), channel_id=1, source_target_pairs={{0,1},{1,2},{2,3},{3,4},{4,5},{5,6},{6,7},{7,8},{8,9},{9,10},{10,1... | collective-permute-start | bytes 294920
  1261.1 15.7 %collective-permute-start.38 = (f32[16,1536]{1,0:T(8,128)S(1)}, f32[16,1536]{1,0:T(8,128)S(1)}, u32[]{:S(2)}, u32[]{:S(2)}) collective-permute-start(f32[16,1536]{1,0:T(8,128)S(1)} %copy-done.47), channel_id=1, source_target_pairs={{0,7},{1,8},{2,9},{3,10},{4,11},{5,12},{6,13},{7,14},{8,15},{9,16}... | collective-permute-start | bytes 294920
  1268.1 12.1 collective-permute-start.37
  1269.4 18.5 %collective-permute-start.36 = (f32[16,1536]{1,0:T(8,128)S(1)}, f32[16,1536]{1,0:T(8,128)S(1)}, u32[]{:S(2)}, u32[]{:S(2)}) collective-permute-start(f32[16,1536]{1,0:T(8,128)S(1)} %copy-done.47), channel_id=1, source_target_pairs={{0,5},{1,6},{2,7},{3,8},{4,9},{5,10},{6,11},{7,12},{8,13},{9,14},{... | collective-permute-start | bytes 294920
  1271.3 16.6 %collective-permute-start.35 = (f32[16,1536]{1,0:T(8,128)S(1)}, f32[16,1536]{1,0:T(8,128)S(1)}, u32[]{:S(2)}, u32[]{:S(2)}) collective-permute-start(f32[16,1536]{1,0:T(8,128)S(1)} %copy-done.47), channel_id=1, source_target_pairs={{0,4},{1,5},{2,6},{3,7},{4,8},{5,9},{6,10},{7,11},{8,12},{9,13},{1... | collective-permute-start | bytes 294920
  1273.8 14.2 %collective-permute-start.34 = (f32[16,1536]{1,0:T(8,128)S(1)}, f32[16,1536]{1,0:T(8,128)}, u32[]{:S(2)}, u32[]{:S(2)}) collective-permute-start(f32[16,1536]{1,0:T(8,128)S(1)} %copy-done.47), channel_id=1, source_target_pairs={{0,3},{1,4},{2,5},{3,6},{4,7},{5,8},{6,9},{7,10},{8,11},{9,12},{10... | collective-permute-start | bytes 294920
  1276.8 11.2 collective-permute-start.33
  1280.1 8.5 collective-permute-start.32
  (122 other events, 1503.6 us)
Sparse Core Ops, SparseCore 0:
  11.5 59.8 all-gather.18
  74.9 52.6 all-gather.20
  131.0 56.5 all-gather.22
  191.0 52.6 all-gather.24
  1043.5 103.0 reduce-scatter.20
  1151.7 106.4 reduce-scatter.18
where the time goes:
time: 1320 us; the launch traced here: 1310 us
  blocking collectives  544 us (41%)
  local copies, waits for them, and re-layouts  266 us (20%)
  matrix products  253 us (19%)
  starting transfers between devices  125 us (9%)
  other arithmetic  100 us (8%)
  between operations  17.1 us (1%)
    unnamed x3, blocking collectives  218 us
    unnamed x48, starting transfers between devices  124 us
    dot_general x12, matrix products, mixed(): return jnp.einsum(form, left, right, preferred_element_type=jnp.float32)  92.3 us
    all_gather x2, blocking collectives, fetch_layer(): lax.all_gather(qkv_part, 'dp', axis=0, tiled=True)  88.2 us
    all_gather x2, blocking collectives, fetch_layer(): lax.all_gather(outw_part, 'dp', axis=0, tiled=True)  83.1 us
    all_gather x2, blocking collectives, fetch_layer(): lax.all_gather(gain_part, 'dp', axis=1, tiled=True)  79.5 us
    all_gather x2, blocking collectives, fetch_layer(): lax.all_gather(shift_part, 'dp', axis=1, tiled=True)  74.9 us
    dot_general x8, matrix products, back_dot(): lax.dot_general(left, weight, (((1,), (1,)), ((), ())), preferred_element...  58 us
  transfers between devices with their start and end apart: 54, of which 1 were waited for; matrix products, arithmetic and copies ran while one was open for 28% of the time, Pallas kernels for 0%

commit v1 on v0

--- a/solution.py
+++ b/solution.py
@@ -11,6 +11,18 @@
 DECAY = 0.05
 ADAM_EPS = 1e-08
 NORM_EPS = 1e-06
+
+
+def collect(array, axis, dim):
+    ways, here = (lax.axis_size(axis), lax.axis_index(axis))
+    grown, reach = (array, 1)
+    while reach < ways:
+        theirs = lax.ppermute(grown, axis, [(d, d ^ reach) for d in range(ways)])
+        mine_first = jnp.concatenate([grown, theirs], axis=dim)
+        theirs_first = jnp.concatenate([theirs, grown], axis=dim)
+        grown = jnp.where(here & reach == 0, mine_first, theirs_first)
+        reach = 2 * reach
+    return grown
 
 
 def mixed(form, left, right):
@@ -200,7 +212,7 @@
         lax.all_gather(gain_part, "dp", axis=1, tiled=True),
         lax.all_gather(shift_part, "dp", axis=1, tiled=True),
         lax.all_gather(upshift_part, "dp", axis=0, tiled=True),
-        lax.all_gather(qkv_part, "dp", axis=0, tiled=True),
+        collect(qkv_part, "dp", 0),
         lax.all_gather(outw_part, "dp", axis=0, tiled=True),
         lax.all_gather(up_part, "dp", axis=0, tiled=True),
         lax.all_gather(down_part, "dp", axis=0, tiled=True),

time: 1320 us -> 1360 us (1.030)
  waiting for transfers between devices: 2.74 us -> 30.9 us
    ppermute x0 -> x10, waiting for transfers between devices: none -> 28.6 us  [collect(): theirs = lax.ppermute(grown, axis, [(d, d ^ reach) for d in range(ways)])]
    unnamed x308 -> x295, local copies, waits for them, and re-layouts: 57.7 us -> 58 us
  transfers between devices with their start and end apart: 54 -> 64, of which waited for: 1 -> 7; matrix products, arithmetic and copies ran while one was open for 28% -> 27% of each run, Pallas kernels for 0% -> 0%
where the time goes in v1:
time: 1360 us; the launch traced here: 1350 us
  blocking collectives  552 us (41%)
  local copies, waits for them, and re-layouts  266 us (20%)
  matrix products  251 us (18%)
  starting transfers between devices  134 us (10%)
  other arithmetic  101 us (7%)
  waiting for transfers between devices  30.9 us (2%)
  between operations  17.1 us (1%)
    unnamed x3, blocking collectives  216 us
    unnamed x48, starting transfers between devices  125 us
    dot_general x12, matrix products, mixed(): return jnp.einsum(form, left, right, preferred_element_type=jnp.float32)  92.3 us
    all_gather x2, blocking collectives, fetch_again(): lax.all_gather(qkv_part, 'dp', axis=0, tiled=True)  91.9 us
    all_gather x2, blocking collectives, fetch_layer(): lax.all_gather(outw_part, 'dp', axis=0, tiled=True)  83 us
    all_gather x2, blocking collectives, fetch_layer(): lax.all_gather(gain_part, 'dp', axis=1, tiled=True)  82.7 us
    all_gather x2, blocking collectives, fetch_layer(): lax.all_gather(shift_part, 'dp', axis=1, tiled=True)  78.7 us
    dot_general x8, matrix products, back_dot(): lax.dot_general(left, weight, (((1,), (1,)), ((), ())), preferred_element...  58 us
  transfers between devices with their start and end apart: 64, of which 7 were waited for; matrix products, arithmetic and copies ran while one was open for 27% of the time, Pallas kernels for 0%

profile of v1, /device:TPU:0, one launch (start us, length us, event | category | flops | bytes accessed | tf_op | source)
XLA Modules:
  0.0 1351.5 jit_solution(15939547066146576414)
XLA Ops:
  17.2 43.9 %all-gather.6 = bf16[1,2,384]{1,0,2:T(2,128)(2,1)S(1)} all-gather(bf16[1,2,12]{1,0,2:T(2,128)(2,1)S(1)} %get-tuple-element.280), channel_id=8, replica_groups=mesh['dp'=32] {'dp'}, dimensions={2}, use_global_device_ids=true | all-gather | bytes 1584 | tf_op jit(solution)/shard_map/all_gather | solution.py:212
  63.1 37.2 %all-gather.7 = bf16[1,6,384]{1,0,2:T(2,128)(2,1)S(1)} all-gather(bf16[1,6,12]{1,0,2:T(2,128)(2,1)S(1)} %get-tuple-element.282), channel_id=9, replica_groups=mesh['dp'=32] {'dp'}, dimensions={2}, use_global_device_ids=true | all-gather | bytes 4752 | tf_op jit(solution)/shard_map/all_gather | solution.py:213
  100.5 8.8 slice_reduce_fusion
  109.2 38.8 %all-gather = bf16[1,2,384]{1,0,2:T(2,128)(2,1)S(1)} all-gather(bf16[1,2,12]{1,0,2:T(2,128)(2,1)S(1)} %get-tuple-element.281), channel_id=2, replica_groups=mesh['dp'=32] {'dp'}, dimensions={2}, use_global_device_ids=true | all-gather | bytes 1584 | tf_op jit(solution)/shard_map/all_gather | solution.py:212
  150.0 41.7 %all-gather.8 = bf16[1,384,384]{2,0,1:T(2,128)(2,1)} all-gather(bf16[1,12,384]{2,0,1:T(2,128)(2,1)S(1)} %get-tuple-element.277), channel_id=10, replica_groups=mesh['dp'=32] {'dp'}, dimensions={1}, use_global_device_ids=true | all-gather | bytes 304128 | tf_op jit(solution)/shard_map/all_gather | solution.py:216
  193.3 16.8 %multiply_reduce_fusion.14 = f32[6,2,197]{1,2,0:T(8,128)S(1)} fusion(f32[6,2,197]{1,2,0:T(8,128)S(1)} %broadcast_multiply_fusion, bf16[6,2,197,384]{3,1,2,0:T(2,128)(2,1)S(1)} %copy-done.21), kind=kLoop, calls=%fused_computation.98 | loop fusion | flops 3628740 | bytes 1834464 | tf_op jit(solution)/shard_map/reduce_sum | solution.py:46
  210.2 46.1 %all-gather.12 = bf16[1,384,1152]{2,0,1:T(2,128)(2,1)} all-gather(bf16[1,12,1152]{2,0,1:T(2,128)(2,1)S(1)} %copy.402), channel_id=14, replica_groups=mesh['dp'=32] {'dp'}, dimensions={1}, use_global_device_ids=true | all-gather | bytes 912384 | tf_op jit(solution)/shard_map/all_gather | solution.py:230
  256.3 45.7 %all-gather.13 = bf16[1,384,1152]{2,0,1:T(2,128)(2,1)} all-gather(bf16[1,12,1152]{2,0,1:T(2,128)(2,1)S(1)} %copy.415), channel_id=15, replica_groups=mesh['dp'=32] {'dp'}, dimensions={1}, use_global_device_ids=true | all-gather | bytes 912384 | tf_op jit(solution)/shard_map/all_gather | solution.py:230
  304.8 41.3 %all-gather.2 = bf16[1,384,384]{2,0,1:T(2,128)(2,1)} all-gather(bf16[1,12,384]{2,0,1:T(2,128)(2,1)S(1)} %get-tuple-element.278), channel_id=4, replica_groups=mesh['dp'=32] {'dp'}, dimensions={1}, use_global_device_ids=true | all-gather | bytes 304128 | tf_op jit(solution)/shard_map/all_gather | solution.py:216
  353.4 37.0 %all-reduce.22 = (bf16[1536]{0:T(1024)(128)(2,1)S(1)}, bf16[1536]{0:T(1024)(128)(2,1)S(1)}) all-reduce(bf16[1536]{0:T(1024)(128)(2,1)S(1)} %dynamic-update-slice, bf16[1536]{0:T(1024)(128)(2,1)S(1)} %dynamic-update-slice.1), channel_id=6, replica_groups=mesh['dp'=32] {'dp'}, use_global_device_ids=true, to_apply=%add.1 | all-reduce | flops 3072 | bytes 12288
  390.6 41.6 %all-gather.1 = bf16[1,6,384]{1,0,2:T(2,128)(2,1)S(1)} all-gather(bf16[1,6,12]{1,0,2:T(2,128)(2,1)S(1)} %get-tuple-element.283), channel_id=3, replica_groups=mesh['dp'=32] {'dp'}, dimensions={2}, use_global_device_ids=true | all-gather | bytes 4752 | tf_op jit(solution)/shard_map/all_gather | solution.py:213
  458.3 8.3 slice_reduce_fusion.8
  469.7 16.7 %collective-permute-done.4 = bf16[192,1152]{1,0:T(8,128)(2,1)S(1)} collective-permute-done((bf16[192,1152]{1,0:T(8,128)(2,1)S(1)}, bf16[192,1152]{1,0:T(8,128)(2,1)S(1)}, u32[]{:S(2)}, u32[]{:S(2)}) %collective-permute-start.4) | collective-permute-done | bytes 442400 | tf_op jit(solution)/shard_map/ppermute | solution.py:20
  498.2 6.4 copy.375
  509.3 5.0 copy.376
  514.3 6.8 reshape.364
  521.2 6.3 copy.377
  527.4 9.0 fusion.142
  536.5 8.6 fusion.16
  545.8 8.2 convert_bitcast_fusion.3
  557.2 5.2 convert_element_type.199
  569.4 12.0 multiply_convert_fusion.3
  581.5 8.6 fusion.144
  602.6 6.6 copy.383
  613.9 5.0 copy.384
  618.9 6.6 reshape.367
  625.5 6.3 copy.385
  631.8 9.0 fusion.145
  640.9 8.6 fusion.17
  649.5 8.1 convert_bitcast_fusion.2
  660.9 6.5 convert_element_type.218
  674.4 11.7 multiply_convert_fusion.2
  686.1 12.4 fusion.147
  703.4 5.2 multiply_reduce_fusion.2
  716.0 6.6 reshape.370
  722.6 6.4 copy.391
  729.1 11.4 bitcast_convert_fusion.2
  740.4 10.0 multiply_reduce_fusion.1
  750.4 10.7 multiply_convert_fusion.1
  772.7 6.2 reshape.290
  782.1 6.3 reshape.288
  805.5 6.4 multiply_reduce_fusion.3
  814.5 14.5 %fusion.148 = (f32[1536]{0:T(1024)}, bf16[2364,1536]{1,0:T(8,128)(2,1)S(1)}) fusion(f32[2364,1536]{1,0:T(8,128)} %get-tuple-element.291, bf16[1,1536,384]{2,1,0:T(8,128)(2,1)S(1)} %copy-done.122, f32[2364,384]{1,0:T(8,128)S(1)} %get-tuple-element.257), kind=kOutput, calls=%fused_computation.309 | convolution fusion | flops 2829536256 | bytes 26603520 | tf_op jit(solution)/shard_map/dot_general | solution.py:39
  833.9 5.2 multiply_reduce_fusion.4
  849.7 5.1 copy.404
  854.8 10.8 bitcast_convert_fusion
  865.5 10.1 multiply_reduce_fusion
  875.6 10.9 multiply_convert_fusion
  897.2 6.1 reshape.294
  906.5 6.1 reshape.292
  915.8 5.0 reshape.293
  931.3 139.2 %fusion.123 = (f32[16,1152]{1,0:T(8,128)}, f32[16,1152]{1,0:T(8,128)}, f32[16,384]{1,0:T(8,128)}, f32[16,384]{1,0:T(8,128)}, f32[16,1536]{1,0:T(8,128)}, /*index=5*/f32[16,1536]{1,0:T(8,128)}) fusion(f32[384,1152]{1,0:T(8,128)} %fusion.122, f32[384,1152]{1,0:T(8,128)} %fusion.121, f32[384,384]{1,0:T(8,128)S(1)} %copy-done.37, ...), kind=kCustom, calls=%all-reduce-scatter.6 | all-reduce-scatter fusion | flops 3145729 | bytes 9830400
  1079.8 9.9 fusion.120
  1099.5 10.5 multiply_reduce_fusion.5
  1111.3 6.2 collective-permute-start.41
  1117.6 39.6 %all-reduce.21 = (f32[2,384]{1,0:T(2,128)S(1)}, f32[2,384]{1,0:T(2,128)S(1)}, f32[6,384]{1,0:T(8,128)S(1)}, f32[6,384]{1,0:T(8,128)S(1)}, f32[1536]{0:T(1024)S(1)}, /*index=5*/f32[1536]{0:T(1024)S(1)}) all-reduce(f32[2,384]{1,0:T(2,128)S(1)} %pad_maximum_fusion.6, ...), channel_id=17, replica_groups=mesh['dp'=32] {'dp'}, use_global_device_ids=true, to_apply=%region_27.28.clone | all-reduce | flops 9216 | bytes 73728
  1157.5 9.9 fusion.58
  1167.5 8.4 add_multiply_fusion
  1176.0 9.1 fusion.32
  1226.8 5.8 copy.432
  1238.7 5.8 copy.433
  1298.4 5.4 collective-permute-start.51
  1305.1 7.0 collective-permute-start.48
  1332.7 6.3 concatenate.94
  (567 shorter events, 347.5 us)
Async XLA Ops:
  7.2 562.2 %all-gather.19.cloned.1.call-start = ((), (), s32[]{:S(2)}) async-start(), calls=%async_computation.4 | async-start | bytes 2433024 | tf_op jit(solution)/shard_map/all_gather | solution.py:217
  9.1 572.4 %all-gather.21.cloned.1.call-start = ((), (), s32[]{:S(2)}) async-start(), calls=%async_computation.5 | async-start | bytes 1216512 | tf_op jit(solution)/shard_map/all_gather | solution.py:218
  10.8 663.6 %all-gather.23.cloned.1.call-start = ((), (), s32[]{:S(2)}) async-start(), calls=%async_computation.6 | async-start | bytes 2433024 | tf_op jit(solution)/shard_map/all_gather | solution.py:217
  11.5 674.6 %all-gather.25.cloned.1.call-start = ((), (), s32[]{:S(2)}) async-start(), calls=%async_computation.7 | async-start | bytes 1216512 | tf_op jit(solution)/shard_map/all_gather | solution.py:218
  12.5 428.6 %collective-permute-start = (bf16[12,1152]{1,0:T(8,128)(2,1)S(1)}, bf16[12,1152]{1,0:T(8,128)(2,1)S(1)}, u32[]{:S(2)}, u32[]{:S(2)}) collective-permute-start(bf16[12,1152]{1,0:T(8,128)(2,1)S(1)} %get-tuple-element.269), channel_id=1, source_target_pairs={{0,1},{1,0},{2,3},{3,2},{4,5},{5,4},{6,7},{7,6},{8,9},{9,8},{10,11... | collective-permute-start | bytes 82952 | tf_op jit(solution)/shard_map/ppermute | solution.py:20
  13.1 428.1 %collective-permute-start.5 = (bf16[12,1152]{1,0:T(8,128)(2,1)S(1)}, bf16[12,1152]{1,0:T(8,128)(2,1)S(1)}, u32[]{:S(2)}, u32[]{:S(2)}) collective-permute-start(bf16[12,1152]{1,0:T(8,128)(2,1)S(1)} %get-tuple-element.270), channel_id=1, source_target_pairs={{0,1},{1,0},{2,3},{3,2},{4,5},{5,4},{6,7},{7,6},{8,9},{9,8},{10,11... | collective-permute-start | bytes 82952 | tf_op jit(solution)/shard_map/ppermute | solution.py:20
  13.2 1329.2 %reduce-scatter.21.cloned.1.call-start = ((), (), s32[]{:S(2)}) async-start(), calls=%async_computation.3 | async-start | bytes 2433024 | tf_op jit(solution)/shard_map/reduce_scatter | solution.py:246
  441.1 4.8 collective-permute-start.1
  441.2 5.2 collective-permute-start.6
  445.9 5.1 collective-permute-start.2
  446.5 5.7 collective-permute-start.7
  451.1 7.1 collective-permute-start.3
  452.3 14.4 %collective-permute-start.8 = (bf16[96,1152]{1,0:T(8,128)(2,1)S(1)}, bf16[96,1152]{1,0:T(8,128)(2,1)S(1)}, u32[]{:S(2)}, u32[]{:S(2)}) collective-permute-start(bf16[96,1152]{1,0:T(8,128)(2,1)S(1)} %maximum_select_fusion.7), channel_id=1, source_target_pairs={{0,8},{1,9},{2,10},{3,11},{4,12},{5,13},{6,14},{7,15},{8,0},{9,1},... | collective-permute-start | bytes 663560 | tf_op jit(solution)/shard_map/ppermute | solution.py:20
  458.2 28.2 %collective-permute-start.4 = (bf16[192,1152]{1,0:T(8,128)(2,1)S(1)}, bf16[192,1152]{1,0:T(8,128)(2,1)S(1)}, u32[]{:S(2)}, u32[]{:S(2)}) collective-permute-start(bf16[192,1152]{1,0:T(8,128)(2,1)S(1)} %maximum_select_fusion.4), channel_id=1, source_target_pairs={{0,16},{1,17},{2,18},{3,19},{4,20},{5,21},{6,22},{7,23},{8,24},{9,... | collective-permute-start | bytes 1327112 | tf_op jit(solution)/shard_map/ppermute | solution.py:20
  466.8 124.2 %collective-permute-start.9 = (bf16[192,1152]{1,0:T(8,128)(2,1)S(1)}, bf16[192,1152]{1,0:T(8,128)(2,1)S(1)}, u32[]{:S(2)}, u32[]{:S(2)}) collective-permute-start(bf16[192,1152]{1,0:T(8,128)(2,1)S(1)} %maximum_select_fusion.5), channel_id=1, source_target_pairs={{0,16},{1,17},{2,18},{3,19},{4,20},{5,21},{6,22},{7,23},{8,24},{9,... | collective-permute-start | bytes 1327112 | tf_op jit(solution)/shard_map/ppermute | solution.py:20
  1071.2 120.0 %collective-permute-start.40 = (f32[16,384]{1,0:T(8,128)}, f32[16,384]{1,0:T(8,128)S(1)}, u32[]{:S(2)}, u32[]{:S(2)}) collective-permute-start(f32[16,384]{1,0:T(8,128)} %get-tuple-element.228), channel_id=1, source_target_pairs={{0,7},{1,8},{2,9},{3,10},{4,11},{5,12},{6,13},{7,14},{8,15},{9,16}... | collective-permute-start | bytes 73736
  1072.5 122.2 %collective-permute-start.39 = (f32[16,384]{1,0:T(8,128)}, f32[16,384]{1,0:T(8,128)S(1)}, u32[]{:S(2)}, u32[]{:S(2)}) collective-permute-start(f32[16,384]{1,0:T(8,128)} %get-tuple-element.228), channel_id=1, source_target_pairs={{0,6},{1,7},{2,8},{3,9},{4,10},{5,11},{6,12},{7,13},{8,14},{9,15},... | collective-permute-start | bytes 73736
  1075.7 123.0 %collective-permute-start.38 = (f32[16,384]{1,0:T(8,128)}, f32[16,384]{1,0:T(8,128)S(1)}, u32[]{:S(2)}, u32[]{:S(2)}) collective-permute-start(f32[16,384]{1,0:T(8,128)} %get-tuple-element.228), channel_id=1, source_target_pairs={{0,5},{1,6},{2,7},{3,8},{4,9},{5,10},{6,11},{7,12},{8,13},{9,14},{... | collective-permute-start | bytes 73736
  1089.8 252.6 %reduce-scatter.19.cloned.1.call-start = ((), (), s32[]{:S(2)}) async-start(), calls=%async_computation.2 | async-start | bytes 2433024 | tf_op jit(solution)/shard_map/reduce_scatter | solution.py:246
  1110.0 75.8 %collective-permute-start.33 = (f32[12,384]{1,0:T(8,128)S(1)}, f32[12,384]{1,0:T(8,128)S(1)}, u32[]{:S(2)}, u32[]{:S(2)}) collective-permute-start(f32[12,384]{1,0:T(8,128)S(1)} %slice.226), channel_id=1, source_target_pairs={{0,8},{1,9},{2,10},{3,11},{4,12},{5,13},{6,14},{7,15},{8,16},{9,17... | collective-permute-start | bytes 55304
  1111.3 78.6 %collective-permute-start.41 = (f32[12,384]{1,0:T(8,128)S(1)}, f32[12,384]{1,0:T(8,128)S(1)}, u32[]{:S(2)}, u32[]{:S(2)}) collective-permute-start(f32[12,384]{1,0:T(8,128)S(1)} %slice.227), channel_id=1, source_target_pairs={{0,8},{1,9},{2,10},{3,11},{4,12},{5,13},{6,14},{7,15},{8,16},{9,17... | collective-permute-start | bytes 55304
  1185.8 17.4 %collective-permute-start.37 = (f32[16,384]{1,0:T(8,128)S(1)}, f32[16,384]{1,0:T(8,128)S(1)}, u32[]{:S(2)}, u32[]{:S(2)}) collective-permute-start(f32[16,384]{1,0:T(8,128)S(1)} %copy-done.57), channel_id=1, source_target_pairs={{0,4},{1,5},{2,6},{3,7},{4,8},{5,9},{6,10},{7,11},{8,12},{9,13},{1... | collective-permute-start | bytes 73736
  1189.9 15.6 %collective-permute-start.36 = (f32[16,384]{1,0:T(8,128)S(1)}, f32[16,384]{1,0:T(8,128)S(1)}, u32[]{:S(2)}, u32[]{:S(2)}) collective-permute-start(f32[16,384]{1,0:T(8,128)S(1)} %copy-done.57), channel_id=1, source_target_pairs={{0,3},{1,4},{2,5},{3,6},{4,7},{5,8},{6,9},{7,10},{8,11},{9,12},{10... | collective-permute-start | bytes 73736
  1191.2 16.2 %collective-permute-start.35 = (f32[16,384]{1,0:T(8,128)S(1)}, f32[16,384]{1,0:T(8,128)S(1)}, u32[]{:S(2)}, u32[]{:S(2)}) collective-permute-start(f32[16,384]{1,0:T(8,128)S(1)} %copy-done.57), channel_id=1, source_target_pairs={{0,2},{1,3},{2,4},{3,5},{4,6},{5,7},{6,8},{7,9},{8,10},{9,11},{10,... | collective-permute-start | bytes 73736
  1194.7 16.3 %collective-permute-start.34 = (f32[16,384]{1,0:T(8,128)S(1)}, f32[16,384]{1,0:T(8,128)S(1)}, u32[]{:S(2)}, u32[]{:S(2)}) collective-permute-start(f32[16,384]{1,0:T(8,128)S(1)} %copy-done.57), channel_id=1, source_target_pairs={{0,1},{1,2},{2,3},{3,4},{4,5},{5,6},{6,7},{7,8},{8,9},{9,10},{10,1... | collective-permute-start | bytes 73736
  1198.7 14.2 %collective-permute-start.32 = (f32[16,384]{1,0:T(8,128)S(1)}, f32[16,384]{1,0:T(8,128)S(1)}, u32[]{:S(2)}, u32[]{:S(2)}) collective-permute-start(f32[16,384]{1,0:T(8,128)S(1)} %copy-done.56), channel_id=1, source_target_pairs={{0,7},{1,8},{2,9},{3,10},{4,11},{5,12},{6,13},{7,14},{8,15},{9,16}... | collective-permute-start | bytes 73736
  1203.2 14.2 %collective-permute-start.31 = (f32[16,384]{1,0:T(8,128)S(1)}, f32[16,384]{1,0:T(8,128)S(1)}, u32[]{:S(2)}, u32[]{:S(2)}) collective-permute-start(f32[16,384]{1,0:T(8,128)S(1)} %copy-done.56), channel_id=1, source_target_pairs={{0,6},{1,7},{2,8},{3,9},{4,10},{5,11},{6,12},{7,13},{8,14},{9,15},... | collective-permute-start | bytes 73736
  1205.6 13.1 collective-permute-start.30
  1207.4 12.6 collective-permute-start.29
  1211.0 34.6 %collective-permute-start.28 = (f32[16,384]{1,0:T(8,128)S(1)}, f32[16,384]{1,0:T(8,128)S(1)}, u32[]{:S(2)}, u32[]{:S(2)}) collective-permute-start(f32[16,384]{1,0:T(8,128)S(1)} %copy-done.56), channel_id=1, source_target_pairs={{0,3},{1,4},{2,5},{3,6},{4,7},{5,8},{6,9},{7,10},{8,11},{9,12},{10... | collective-permute-start | bytes 73736
  1212.9 35.4 %collective-permute-start.27 = (f32[16,384]{1,0:T(8,128)S(1)}, f32[16,384]{1,0:T(8,128)S(1)}, u32[]{:S(2)}, u32[]{:S(2)}) collective-permute-start(f32[16,384]{1,0:T(8,128)S(1)} %copy-done.56), channel_id=1, source_target_pairs={{0,2},{1,3},{2,4},{3,5},{4,6},{5,7},{6,8},{7,9},{8,10},{9,11},{10,... | collective-permute-start | bytes 73736
  1217.4 33.5 %collective-permute-start.26 = (f32[16,384]{1,0:T(8,128)S(1)}, f32[16,384]{1,0:T(8,128)S(1)}, u32[]{:S(2)}, u32[]{:S(2)}) collective-permute-start(f32[16,384]{1,0:T(8,128)S(1)} %copy-done.56), channel_id=1, source_target_pairs={{0,1},{1,2},{2,3},{3,4},{4,5},{5,6},{6,7},{7,8},{8,9},{9,10},{10,1... | collective-permute-start | bytes 73736
  1218.7 35.8 %collective-permute-start.17 = (f32[12,1152]{1,0:T(8,128)S(1)}, f32[12,1152]{1,0:T(8,128)S(1)}, u32[]{:S(2)}, u32[]{:S(2)}) collective-permute-start(f32[12,1152]{1,0:T(8,128)S(1)} %slice.224), channel_id=1, source_target_pairs={{0,8},{1,9},{2,10},{3,11},{4,12},{5,13},{6,14},{7,15},{8,16},{9,17... | collective-permute-start | bytes 165896
  1220.1 35.9 %collective-permute-start.25 = (f32[12,1152]{1,0:T(8,128)S(1)}, f32[12,1152]{1,0:T(8,128)S(1)}, u32[]{:S(2)}, u32[]{:S(2)}) collective-permute-start(f32[12,1152]{1,0:T(8,128)S(1)} %slice.225), channel_id=1, source_target_pairs={{0,8},{1,9},{2,10},{3,11},{4,12},{5,13},{6,14},{7,15},{8,16},{9,17... | collective-permute-start | bytes 165896
  1245.6 12.2 collective-permute-start.24
  1248.3 13.4 collective-permute-start.23
  1250.9 12.1 collective-permute-start.22
  1254.5 11.7 collective-permute-start.21
  1256.0 11.5 collective-permute-start.20
  1257.8 12.3 collective-permute-start.19
  1261.7 9.7 collective-permute-start.18
  1263.1 11.2 collective-permute-start.16
  1266.2 11.2 collective-permute-start.15
  1267.5 11.2 collective-permute-start.14
  1270.1 13.7 %collective-permute-start.13 = (f32[16,1152]{1,0:T(8,128)S(1)}, f32[16,1152]{1,0:T(8,128)S(1)}, u32[]{:S(2)}, u32[]{:S(2)}) collective-permute-start(f32[16,1152]{1,0:T(8,128)S(1)} %copy-done.48), channel_id=1, source_target_pairs={{0,4},{1,5},{2,6},{3,7},{4,8},{5,9},{6,10},{7,11},{8,12},{9,13},{1... | collective-permute-start | bytes 221192
  1271.4 14.9 %collective-permute-start.12 = (f32[16,1152]{1,0:T(8,128)S(1)}, f32[16,1152]{1,0:T(8,128)S(1)}, u32[]{:S(2)}, u32[]{:S(2)}) collective-permute-start(f32[16,1152]{1,0:T(8,128)S(1)} %copy-done.48), channel_id=1, source_target_pairs={{0,3},{1,4},{2,5},{3,6},{4,7},{5,8},{6,9},{7,10},{8,11},{9,12},{10... | collective-permute-start | bytes 221192
  1274.2 13.7 %collective-permute-start.11 = (f32[16,1152]{1,0:T(8,128)S(1)}, f32[16,1152]{1,0:T(8,128)S(1)}, u32[]{:S(2)}, u32[]{:S(2)}) collective-permute-start(f32[16,1152]{1,0:T(8,128)S(1)} %copy-done.48), channel_id=1, source_target_pairs={{0,2},{1,3},{2,4},{3,5},{4,6},{5,7},{6,8},{7,9},{8,10},{9,11},{10,... | collective-permute-start | bytes 221192
  1277.4 12.2 collective-permute-start.10
  1278.7 13.5 %collective-permute-start.49 = (f32[12,1536]{1,0:T(8,128)S(1)}, f32[12,1536]{1,0:T(8,128)S(1)}, u32[]{:S(2)}, u32[]{:S(2)}) collective-permute-start(f32[12,1536]{1,0:T(8,128)S(1)} %slice.228), channel_id=1, source_target_pairs={{0,8},{1,9},{2,10},{3,11},{4,12},{5,13},{6,14},{7,15},{8,16},{9,17... | collective-permute-start | bytes 221192
  1283.8 14.6 %collective-permute-start.56 = (f32[16,1536]{1,0:T(8,128)S(1)}, f32[16,1536]{1,0:T(8,128)S(1)}, u32[]{:S(2)}, u32[]{:S(2)}) collective-permute-start(f32[16,1536]{1,0:T(8,128)S(1)} %copy-done.47), channel_id=1, source_target_pairs={{0,7},{1,8},{2,9},{3,10},{4,11},{5,12},{6,13},{7,14},{8,15},{9,16}... | collective-permute-start | bytes 294920
  1286.3 17.4 %collective-permute-start.55 = (f32[16,1536]{1,0:T(8,128)S(1)}, f32[16,1536]{1,0:T(8,128)S(1)}, u32[]{:S(2)}, u32[]{:S(2)}) collective-permute-start(f32[16,1536]{1,0:T(8,128)S(1)} %copy-done.47), channel_id=1, source_target_pairs={{0,6},{1,7},{2,8},{3,9},{4,10},{5,11},{6,12},{7,13},{8,14},{9,15},... | collective-permute-start | bytes 294920
  1287.9 17.2 %collective-permute-start.54 = (f32[16,1536]{1,0:T(8,128)S(1)}, f32[16,1536]{1,0:T(8,128)S(1)}, u32[]{:S(2)}, u32[]{:S(2)}) collective-permute-start(f32[16,1536]{1,0:T(8,128)S(1)} %copy-done.47), channel_id=1, source_target_pairs={{0,5},{1,6},{2,7},{3,8},{4,9},{5,10},{6,11},{7,12},{8,13},{9,14},{... | collective-permute-start | bytes 294920
  1289.5 22.6 %collective-permute-start.53 = (f32[16,1536]{1,0:T(8,128)S(1)}, f32[16,1536]{1,0:T(8,128)S(1)}, u32[]{:S(2)}, u32[]{:S(2)}) collective-permute-start(f32[16,1536]{1,0:T(8,128)S(1)} %copy-done.47), channel_id=1, source_target_pairs={{0,4},{1,5},{2,6},{3,7},{4,8},{5,9},{6,10},{7,11},{8,12},{9,13},{1... | collective-permute-start | bytes 294920
  1292.2 3.8 collective-permute-start.57
  1296.0 17.5 %collective-permute-start.52 = (f32[16,1536]{1,0:T(8,128)S(1)}, f32[16,1536]{1,0:T(8,128)S(1)}, u32[]{:S(2)}, u32[]{:S(2)}) collective-permute-start(f32[16,1536]{1,0:T(8,128)S(1)} %copy-done.47), channel_id=1, source_target_pairs={{0,3},{1,4},{2,5},{3,6},{4,7},{5,8},{6,9},{7,10},{8,11},{9,12},{10... | collective-permute-start | bytes 294920
  1298.4 17.0 %collective-permute-start.51 = (f32[16,1536]{1,0:T(8,128)S(1)}, f32[16,1536]{1,0:T(8,128)S(1)}, u32[]{:S(2)}, u32[]{:S(2)}) collective-permute-start(f32[16,1536]{1,0:T(8,128)S(1)} %copy-done.47), channel_id=1, source_target_pairs={{0,2},{1,3},{2,4},{3,5},{4,6},{5,7},{6,8},{7,9},{8,10},{9,11},{10,... | collective-permute-start | bytes 294920
  1303.8 14.1 %collective-permute-start.50 = (f32[16,1536]{1,0:T(8,128)S(1)}, f32[16,1536]{1,0:T(8,128)S(1)}, u32[]{:S(2)}, u32[]{:S(2)}) collective-permute-start(f32[16,1536]{1,0:T(8,128)S(1)} %copy-done.47), channel_id=1, source_target_pairs={{0,1},{1,2},{2,3},{3,4},{4,5},{5,6},{6,7},{7,8},{8,9},{9,10},{10,1... | collective-permute-start | bytes 294920
  1305.1 15.7 %collective-permute-start.48 = (f32[16,1536]{1,0:T(8,128)S(1)}, f32[16,1536]{1,0:T(8,128)S(1)}, u32[]{:S(2)}, u32[]{:S(2)}) collective-permute-start(f32[16,1536]{1,0:T(8,128)S(1)} %copy-done.46), channel_id=1, source_target_pairs={{0,7},{1,8},{2,9},{3,10},{4,11},{5,12},{6,13},{7,14},{8,15},{9,16}... | collective-permute-start | bytes 294920
  1312.2 12.0 collective-permute-start.47
  1313.5 18.5 %collective-permute-start.46 = (f32[16,1536]{1,0:T(8,128)S(1)}, f32[16,1536]{1,0:T(8,128)S(1)}, u32[]{:S(2)}, u32[]{:S(2)}) collective-permute-start(f32[16,1536]{1,0:T(8,128)S(1)} %copy-done.46), channel_id=1, source_target_pairs={{0,5},{1,6},{2,7},{3,8},{4,9},{5,10},{6,11},{7,12},{8,13},{9,14},{... | collective-permute-start | bytes 294920
  1315.4 16.6 %collective-permute-start.45 = (f32[16,1536]{1,0:T(8,128)S(1)}, f32[16,1536]{1,0:T(8,128)S(1)}, u32[]{:S(2)}, u32[]{:S(2)}) collective-permute-start(f32[16,1536]{1,0:T(8,128)S(1)} %copy-done.46), channel_id=1, source_target_pairs={{0,4},{1,5},{2,6},{3,7},{4,8},{5,9},{6,10},{7,11},{8,12},{9,13},{1... | collective-permute-start | bytes 294920
  1317.9 14.1 %collective-permute-start.44 = (f32[16,1536]{1,0:T(8,128)S(1)}, f32[16,1536]{1,0:T(8,128)}, u32[]{:S(2)}, u32[]{:S(2)}) collective-permute-start(f32[16,1536]{1,0:T(8,128)S(1)} %copy-done.46), channel_id=1, source_target_pairs={{0,3},{1,4},{2,5},{3,6},{4,7},{5,8},{6,9},{7,10},{8,11},{9,12},{10... | collective-permute-start | bytes 294920
  1320.9 11.2 collective-permute-start.43
  1324.2 8.5 collective-permute-start.42
  (125 other events, 4049.2 us)
Sparse Core Ops, SparseCore 0:
  11.5 60.0 all-gather.18
  75.1 52.8 all-gather.20
  131.5 57.1 all-gather.22
  192.0 55.4 all-gather.24
  1089.9 100.6 reduce-scatter.20
  1195.8 106.5 reduce-scatter.18
